TPU v7x, 32 devices: a whole 2x2x4 slice. The times are simulated.
32 devices in a mesh: grp: 2 (over y), dev: 16 (over z, x, core).
Axes of the slice: x: 2, y: 2, z: 4, core: 2. Of those that a mesh axis runs over, the one named last changes fastest.
Arguments:
- queries: float32 [128, 1024], P(('grp', 'dev')), may hold values from -4.5 to 4.5
- documents: float32 [4096, 1024], P(('grp', 'dev')), may hold values from -0.75 to 0.75
- doc_codes: int32 [4096, 128], P(('grp', 'dev')), may hold values from 0 to 255
- codebook: float32 [256, 1024], replicated, may hold values from -0.75 to 0.75
- candidate_owner: int32 [128, 32], P(('grp', 'dev')), may hold values from 0 to 31, all different within a row; in each aligned block of 4 rows (0 to 3, 4 to 7, ...) at most 4 rows name the same one
- candidate_local: int32 [128, 32], P(('grp', 'dev')), may hold values from 0 to 127
Outputs:
- codebook_gradient: float32 [256, 1024], P('dev', 'grp')
- query_loss: float32 [128], P(('grp', 'dev'))
Inputs may be any that keep to these rules, and one draw needn't show every extreme that they name: `candidate_owner`: each query names 32 different owners; among one device's 4 queries no owner is named more than 4 times, and in some device's queries one owner is named exactly 4 times.
All inputs are finite; a program needn't handle non-finite values.
Results may differ from a plain program's by a relative error of at most 0.0003.
Values sent between devices are 32-bit elements; how exact they have to be, the bound alone decides.
No kernel may reach another device: no remote copies, remote signals or barrier semaphores. Data moves between devices by JAX's collectives and lax.ppermute only.
A program may use at most 192 MiB of HBM per device.

v0:
```python
import jax
import jax.numpy as jnp
from jax import lax
from jax.sharding import PartitionSpec as P

D = 1024
M = 128
K = 256
C = 32
SUB = 8


def slot_positions(candidate_owner, capacity):
    owner_flat = candidate_owner.reshape(-1)
    ordinal = jnp.arange(owner_flat.shape[0], dtype=jnp.int32)
    earlier = (owner_flat[None, :] == owner_flat[:, None]) & (ordinal[None, :] < ordinal[:, None])
    rank_inside = jnp.sum(earlier.astype(jnp.int32), axis=1)
    return owner_flat * capacity + rank_inside


def distill(exact_score, student):
    teacher = jax.nn.softmax(exact_score, axis=-1)
    query_loss = jnp.sum(
        teacher * (jax.nn.log_softmax(exact_score, axis=-1) - jax.nn.log_softmax(student, axis=-1)),
        axis=-1,
    )
    weight = jax.nn.softmax(student, axis=-1) - teacher
    return (query_loss, weight)


def code_onehot(code_block):
    return (code_block[:, :, None] == jnp.arange(K, dtype=jnp.int32)[None, None, :]).astype(
        jnp.float32
    )


def fetched_terms(queries, vectors, code_rows, codebook):
    query_count = queries.shape[0]
    exact_score = jnp.einsum("qcd,qd->qc", vectors, queries, precision=lax.Precision.HIGHEST)
    query_parts = queries.reshape(query_count, M, SUB)
    lookup = jnp.einsum(
        "qmj,kmj->qmk", query_parts, codebook.reshape(K, M, SUB), precision=lax.Precision.HIGHEST
    )

    def student_one(pieces):
        code_one, lookup_one = pieces
        return jnp.einsum(
            "cmk,mk->c", code_onehot(code_one), lookup_one, precision=lax.Precision.HIGHEST
        )

    student = lax.map(student_one, (code_rows, lookup))
    query_loss, weight = distill(exact_score, student)

    def table_one(pieces):
        code_one, weight_one = pieces
        return jnp.einsum(
            "cmk,c->mk", code_onehot(code_one), weight_one, precision=lax.Precision.HIGHEST
        )

    weight_table = lax.map(table_one, (code_rows, weight))
    gradient = jnp.einsum(
        "qmk,qmj->kmj", weight_table, query_parts, precision=lax.Precision.HIGHEST
    )
    return (query_loss, gradient.reshape(K, D))


def shards(queries, documents, doc_codes, codebook, candidate_owner, candidate_local):
    groups = lax.axis_size("grp")
    owners = lax.axis_size("dev")
    query_count = queries.shape[0]
    capacity = min(query_count, max(2, 2 * query_count * C // (groups * owners)))
    slot_count = groups * owners * capacity
    positions = slot_positions(candidate_owner, capacity)
    wanted = jnp.zeros((slot_count,), jnp.int32).at[positions].set(candidate_local.reshape(-1))
    asked = lax.all_to_all(
        lax.all_to_all(
            wanted.reshape(groups, owners, capacity), "grp", split_axis=0, concat_axis=0, tiled=True
        ),
        "dev",
        split_axis=1,
        concat_axis=1,
        tiled=True,
    )
    doc_index = asked.reshape(slot_count)
    found_rows = documents[doc_index].reshape(groups, owners, capacity, D)
    found_codes = doc_codes[doc_index].astype(jnp.float32).reshape(groups, owners, capacity, M)
    fetched, fetched_codes = (
        lax.all_to_all(
            lax.all_to_all(found_rows, "grp", split_axis=0, concat_axis=0, tiled=True),
            "dev",
            split_axis=1,
            concat_axis=1,
            tiled=True,
        ),
        lax.all_to_all(
            lax.all_to_all(found_codes, "grp", split_axis=0, concat_axis=0, tiled=True),
            "dev",
            split_axis=1,
            concat_axis=1,
            tiled=True,
        ),
    )
    vectors = fetched.reshape(slot_count, D)[positions].reshape(query_count, C, D)
    code_rows = (
        fetched_codes.reshape(slot_count, M)[positions].astype(jnp.int32).reshape(query_count, C, M)
    )
    query_loss, local_gradient = fetched_terms(queries, vectors, code_rows, codebook)
    partial_sum = lax.psum_scatter(local_gradient, "dev", scatter_dimension=0, tiled=True)
    codebook_gradient = lax.psum_scatter(partial_sum, "grp", scatter_dimension=1, tiled=True)
    return (codebook_gradient, query_loss)


def solution(mesh):
    in_specs = (
        P(("grp", "dev"), None),
        P(("grp", "dev"), None),
        P(("grp", "dev"), None),
        P(),
        P(("grp", "dev"), None),
        P(("grp", "dev"), None),
    )
    out_specs = (P("dev", "grp"), P(("grp", "dev")))
    return jax.shard_map(shards, mesh=mesh, in_specs=in_specs, out_specs=out_specs, check_vma=False)
```

profile of v0, /device:TPU:0, one launch (start us, length us, event | category | flops | bytes accessed | tf_op | source)
XLA Modules:
  0.0 180.2 jit_solution(6461381742338682574)
XLA Ops:
  9.8 1.0 scatter_custom_fusion
  11.0 7.8 %all_to_all.30 = s32[2,16,4]{1,2,0:T(4,128)S(1)} all-to-all(s32[2,16,4]{1,2,0:T(4,128)S(1)} %copy.46), channel_id=1, replica_groups=mesh['grp'=2,'dev'=16] {'grp'}, dimensions={0} | all-to-all | bytes 1024 | tf_op jit(solution)/shard_map/all_to_all | solution.py:76
  18.9 12.2 %all_to_all.31 = s32[2,16,4]{2,0,1:T(2,128)S(1)} all-to-all(s32[2,16,4]{2,0,1:T(2,128)S(1)} %copy.47), channel_id=1, replica_groups=mesh['grp'=2,'dev'=16] {'dev'}, dimensions={1} | all-to-all | bytes 1024 | tf_op jit(solution)/shard_map/all_to_all | solution.py:75
  31.2 1.5 gather_fusion
  32.7 6.5 %all_to_all.32 = f32[2,16,4,128]{3,2,1,0:T(4,128)S(1)} all-to-all(f32[2,16,4,128]{3,2,1,0:T(4,128)S(1)} %bitcast.63), channel_id=1, replica_groups=mesh['grp'=2,'dev'=16] {'grp'}, dimensions={0} | all-to-all | bytes 131072 | tf_op jit(solution)/shard_map/all_to_all | solution.py:96
  39.8 3.5 %all-to-all-start.3 = ((f32[2,16,4,128]{3,2,0,1:T(4,128)}), f32[2,16,4,128]{3,2,0,1:T(4,128)S(1)}, u32[]{:S(2)}, u32[]{:S(2)}) async-start(f32[2,16,4,128]{3,2,0,1:T(4,128)} %copy.49), calls=%async_computation.3 | async-start | bytes 131072 | tf_op jit(solution)/shard_map/all_to_all | solution.py:95
  44.7 1.0 reshape.118
  45.7 4.5 %all-to-all-done.3 = f32[2,16,4,128]{3,2,0,1:T(4,128)S(1)} async-done(((f32[2,16,4,128]{3,2,0,1:T(4,128)}), f32[2,16,4,128]{3,2,0,1:T(4,128)S(1)}, u32[]{:S(2)}, u32[]{:S(2)}) %all-to-all-start.3) | async-done | bytes 65568 | tf_op jit(solution)/shard_map/all_to_all | solution.py:95
  50.2 3.5 %all-to-all-start.4 = ((f32[2,16,4,1024]{3,2,1,0:T(4,128)}), f32[2,16,4,1024]{3,2,1,0:T(4,128)S(1)}, u32[]{:S(2)}, u32[]{:S(2)}) async-start(f32[2,16,4,1024]{3,2,1,0:T(4,128)} %reshape.118), calls=%async_computation.4 | async-start | bytes 1048576 | tf_op jit(solution)/shard_map/all_to_all | solution.py:89
  53.7 1.1 convolution_bitcast_fusion.1
  55.5 6.1 %all-to-all-done.4 = f32[2,16,4,1024]{3,2,1,0:T(4,128)S(1)} async-done(((f32[2,16,4,1024]{3,2,1,0:T(4,128)}), f32[2,16,4,1024]{3,2,1,0:T(4,128)S(1)}, u32[]{:S(2)}, u32[]{:S(2)}) %all-to-all-start.4) | async-done | bytes 524320 | tf_op jit(solution)/shard_map/all_to_all | solution.py:89
  62.5 3.6 %all-to-all-start.5 = ((f32[2,16,4,1024]{3,2,0,1:T(4,128)}), f32[2,16,4,1024]{3,2,0,1:T(4,128)S(1)}, u32[]{:S(2)}, u32[]{:S(2)}) async-start(f32[2,16,4,1024]{3,2,0,1:T(4,128)} %copy.54), calls=%async_computation.5 | async-start | bytes 1048576 | tf_op jit(solution)/shard_map/all_to_all | solution.py:88
  66.1 6.7 %while.20 = (s32[]{:T(128)}, f32[4,32]{1,0:T(4,128)S(1)}, s32[4,32,128]{2,1,0:T(8,128)S(1)}, f32[4,128,256]{2,0,1:T(4,128)S(1)}, s32[]{:T(128)}, /*index=5*/s32[]{:T(128)}) while((s32[]{:T(128)}, f32[4,32]{1,0:T(4,128)S(1)}, s32[4,32,128]{2,1,0:T(8,128)S(1)}, f32[4,128,256]{2,0,1:T(4,128)S(1)}, s32[]{:T(128)}, /*index=5*/s32[]{:T(128)}) %tuple.53), condition=%wide.region_3.4_spmd, body=%wide.region_2.3_spmd.sunk | while | flops 3145698 | bytes 704977 | solution.py:51
  66.3 1.5 select_reduce_fusion.2
  68.0 1.5 select_reduce_fusion.2
  69.7 1.5 select_reduce_fusion.2
  71.4 1.5 select_reduce_fusion.2
  73.0 7.5 %all-to-all-done.5 = f32[2,16,4,1024]{3,2,0,1:T(4,128)S(1)} async-done(((f32[2,16,4,1024]{3,2,0,1:T(4,128)}), f32[2,16,4,1024]{3,2,0,1:T(4,128)S(1)}, u32[]{:S(2)}, u32[]{:S(2)}) %all-to-all-start.5) | async-done | bytes 524320 | tf_op jit(solution)/shard_map/all_to_all | solution.py:88
  83.2 19.7 %while.21 = (s32[]{:T(128)}, f32[4,128,256]{2,0,1:T(4,128)S(1)}, s32[4,32,128]{2,1,0:T(8,128)S(1)}, f32[4,32]{1,0:T(4,128)S(1)}, s32[]{:T(128)}, /*index=5*/s32[]{:T(128)}) while((s32[]{:T(128)}, f32[4,128,256]{2,0,1:T(4,128)S(1)}, s32[4,32,128]{2,1,0:T(8,128)S(1)}, f32[4,32]{1,0:T(4,128)S(1)}, s32[]{:T(128)}, /*index=5*/s32[]{:T(128)}) %tuple.55), condition=%wide.region_9.10_spmd, body=%wide.region_8.9_spmd.sunk | while | flops 13631490 | bytes 2540113 | solution.py:60
  84.1 2.2 %fusion.21 = f32[1,128,256]{2,0,1:T(1,128)S(1)} fusion(pred[32,128,256]{2,1,0:T(32,128)(4,1)S(1)} %iota_compare_fusion.4, f32[4,32]{1,0:T(4,128)S(1)} %get-tuple-element.172, s32[]{:T(128)} %get-tuple-element.163), kind=kOutput, calls=%fused_computation.6.clone.1 | convolution fusion | flops 12582912 | bytes 1180164 | tf_op jit(solution)/shard_map/while/body/eval_jaxpr/cmk,c->mk/dot_general | solution.py:56
  86.2 1.8 %dynamic_update_slice.11 = f32[4,128,256]{2,0,1:T(4,128)S(1)} dynamic-update-slice(f32[4,128,256]{2,0,1:T(4,128)S(1)} %get-tuple-element.164, f32[1,128,256]{2,0,1:T(1,128)S(1)} %fusion.21, s32[]{:T(128)} %get-tuple-element.163, s32[]{:T(128)} %constant.21.clone.1..sunk.1, s32[]{:T(128)} %constant.21.clone.1..sunk.1) | dynamic-update-slice | bytes 262148 | tf_op jit(solution)/shard_map/while/body/jit(dynamic_update_index_in_dim)/dynamic_update_slice | solution.py:60
  88.1 0.9 iota_compare_fusion.4
  89.0 2.2 %fusion.21 = f32[1,128,256]{2,0,1:T(1,128)S(1)} fusion(pred[32,128,256]{2,1,0:T(32,128)(4,1)S(1)} %iota_compare_fusion.4, f32[4,32]{1,0:T(4,128)S(1)} %get-tuple-element.172, s32[]{:T(128)} %get-tuple-element.163), kind=kOutput, calls=%fused_computation.6.clone.1 | convolution fusion | flops 12582912 | bytes 1180164 | tf_op jit(solution)/shard_map/while/body/eval_jaxpr/cmk,c->mk/dot_general | solution.py:56
  91.2 1.8 %dynamic_update_slice.11 = f32[4,128,256]{2,0,1:T(4,128)S(1)} dynamic-update-slice(f32[4,128,256]{2,0,1:T(4,128)S(1)} %get-tuple-element.164, f32[1,128,256]{2,0,1:T(1,128)S(1)} %fusion.21, s32[]{:T(128)} %get-tuple-element.163, s32[]{:T(128)} %constant.21.clone.1..sunk.1, s32[]{:T(128)} %constant.21.clone.1..sunk.1) | dynamic-update-slice | bytes 262148 | tf_op jit(solution)/shard_map/while/body/jit(dynamic_update_index_in_dim)/dynamic_update_slice | solution.py:60
  93.9 2.2 %fusion.21 = f32[1,128,256]{2,0,1:T(1,128)S(1)} fusion(pred[32,128,256]{2,1,0:T(32,128)(4,1)S(1)} %iota_compare_fusion.4, f32[4,32]{1,0:T(4,128)S(1)} %get-tuple-element.172, s32[]{:T(128)} %get-tuple-element.163), kind=kOutput, calls=%fused_computation.6.clone.1 | convolution fusion | flops 12582912 | bytes 1180164 | tf_op jit(solution)/shard_map/while/body/eval_jaxpr/cmk,c->mk/dot_general | solution.py:56
  96.1 1.8 %dynamic_update_slice.11 = f32[4,128,256]{2,0,1:T(4,128)S(1)} dynamic-update-slice(f32[4,128,256]{2,0,1:T(4,128)S(1)} %get-tuple-element.164, f32[1,128,256]{2,0,1:T(1,128)S(1)} %fusion.21, s32[]{:T(128)} %get-tuple-element.163, s32[]{:T(128)} %constant.21.clone.1..sunk.1, s32[]{:T(128)} %constant.21.clone.1..sunk.1) | dynamic-update-slice | bytes 262148 | tf_op jit(solution)/shard_map/while/body/jit(dynamic_update_index_in_dim)/dynamic_update_slice | solution.py:60
  98.9 2.2 %fusion.21 = f32[1,128,256]{2,0,1:T(1,128)S(1)} fusion(pred[32,128,256]{2,1,0:T(32,128)(4,1)S(1)} %iota_compare_fusion.4, f32[4,32]{1,0:T(4,128)S(1)} %get-tuple-element.172, s32[]{:T(128)} %get-tuple-element.163), kind=kOutput, calls=%fused_computation.6.clone.1 | convolution fusion | flops 12582912 | bytes 1180164 | tf_op jit(solution)/shard_map/while/body/eval_jaxpr/cmk,c->mk/dot_general | solution.py:56
  101.0 1.8 %dynamic_update_slice.11 = f32[4,128,256]{2,0,1:T(4,128)S(1)} dynamic-update-slice(f32[4,128,256]{2,0,1:T(4,128)S(1)} %get-tuple-element.164, f32[1,128,256]{2,0,1:T(1,128)S(1)} %fusion.21, s32[]{:T(128)} %get-tuple-element.163, s32[]{:T(128)} %constant.21.clone.1..sunk.1, s32[]{:T(128)} %constant.21.clone.1..sunk.1) | dynamic-update-slice | bytes 262148 | tf_op jit(solution)/shard_map/while/body/jit(dynamic_update_index_in_dim)/dynamic_update_slice | solution.py:60
  102.9 1.4 convolution_bitcast_fusion
  104.3 1.3 copy.58
  105.7 55.9 %reduce-scatter.3.cloned.1.call-done = f32[16,1024]{1,0:T(8,128)} async-done(((f32[256,1024]{1,0:T(8,128)}), f32[16,1024]{1,0:T(8,128)}) %reduce-scatter.3.cloned.1.call-update) | async-done | bytes 65552 | tf_op jit(solution)/shard_map/reduce_scatter | solution.py:108
  161.6 11.7 %reduce-scatter.5.cloned.1.call-done = f32[16,512]{1,0:T(8,128)} async-done(((f32[16,1024]{1,0:T(8,128)}), f32[16,512]{1,0:T(8,128)}) %reduce-scatter.5.cloned.1.call-update) | async-done | bytes 32784 | tf_op jit(solution)/shard_map/reduce_scatter | solution.py:109
  (70 shorter events, 12.6 us)
Async XLA Ops:
  7.2 36.7 %copy-start = (f32[128,1024]{1,0:T(8,128)S(1)}, f32[128,1024]{1,0:T(8,128)}, u32[]{:S(2)}) copy-start(f32[128,1024]{1,0:T(8,128)} %param.12) | copy-start | bytes 1572868
  7.2 36.2 %copy-start.3 = (f32[4,1024]{1,0:T(4,128)S(1)}, f32[4,1024]{1,0:T(4,128)}, u32[]{:S(2)}) copy-start(f32[4,1024]{1,0:T(4,128)} %param.11) | copy-start | bytes 49156
  7.2 36.4 %copy-start.1 = (f32[256,1024]{1,0:T(8,128)S(1)}, f32[256,1024]{1,0:T(8,128)}, u32[]{:S(2)}) copy-start(f32[256,1024]{1,0:T(8,128)} %param.14) | copy-start | bytes 3145732
  39.8 10.4 %all-to-all-start.3 = ((f32[2,16,4,128]{3,2,0,1:T(4,128)}), f32[2,16,4,128]{3,2,0,1:T(4,128)S(1)}, u32[]{:S(2)}, u32[]{:S(2)}) async-start(f32[2,16,4,128]{3,2,0,1:T(4,128)} %copy.49), calls=%async_computation.3 | async-start | bytes 131072 | tf_op jit(solution)/shard_map/all_to_all | solution.py:95
  50.2 11.5 %all-to-all-start.4 = ((f32[2,16,4,1024]{3,2,1,0:T(4,128)}), f32[2,16,4,1024]{3,2,1,0:T(4,128)S(1)}, u32[]{:S(2)}, u32[]{:S(2)}) async-start(f32[2,16,4,1024]{3,2,1,0:T(4,128)} %reshape.118), calls=%async_computation.4 | async-start | bytes 1048576 | tf_op jit(solution)/shard_map/all_to_all | solution.py:89
  62.5 18.0 %all-to-all-start.5 = ((f32[2,16,4,1024]{3,2,0,1:T(4,128)}), f32[2,16,4,1024]{3,2,0,1:T(4,128)S(1)}, u32[]{:S(2)}, u32[]{:S(2)}) async-start(f32[2,16,4,1024]{3,2,0,1:T(4,128)} %copy.54), calls=%async_computation.5 | async-start | bytes 1048576 | tf_op jit(solution)/shard_map/all_to_all | solution.py:88
  66.1 95.5 %reduce-scatter.3.cloned.1.call-start = ((), (), s32[]{:S(2)}) async-start(), calls=%async_computation.8 | async-start | bytes 1114112 | tf_op jit(solution)/shard_map/reduce_scatter | solution.py:108
  80.7 2.5 %copy-start.2 = (f32[4,128,256]{2,0,1:T(4,128)S(1)}, f32[4,128,256]{2,0,1:T(4,128)}, u32[]{:S(2)}) copy-start(f32[4,128,256]{2,0,1:T(4,128)} %custom-call.9) | copy-start | bytes 1572868
  105.6 67.8 %reduce-scatter.5.cloned.1.call-start = ((), (), s32[]{:S(2)}) async-start(), calls=%async_computation.9 | async-start | bytes 98304 | tf_op jit(solution)/shard_map/reduce_scatter | solution.py:109
Sparse Core Ops, SparseCore 0:
  105.7 55.8 reduce-scatter.2
  164.5 8.8 reduce-scatter.4
where the time goes:
time: 181 us; the launch traced here: 180 us
  waiting for transfers between devices  85.9 us (47%)
  blocking collectives  26.5 us (15%)
  local copies, waits for them, and re-layouts  19.3 us (11%)
  between operations  14.3 us (8%)
  matrix products  11.8 us (7%)
  other arithmetic  11.6 us (6%)
  starting transfers between devices  10.6 us (6%)
    reduce_scatter x1, waiting for transfers between devices, shards(): lax.psum_scatter(local_gradient, 'dev', scatter_dimension=0, tiled=True)  55.9 us
    all_to_all x1, blocking collectives, shards(): lax.all_to_all(lax.all_to_all(wanted.reshape(groups, owners, capacity), '...  12.2 us
    reduce_scatter x1, waiting for transfers between devices, shards(): lax.psum_scatter(partial_sum, 'grp', scatter_dimension=1, tiled=True)  11.7 us
    dot_general x4, matrix products, table_one(): jnp.einsum('cmk,c->mk', code_onehot(code_one), weight_one, precision=lax....  8.72 us
    all_to_all x1, blocking collectives, shards(): lax.all_to_all(wanted.reshape(groups, owners, capacity), 'grp', split_axi...  7.82 us
    all_to_all x1, waiting for transfers between devices, shards(): lax.all_to_all(lax.all_to_all(found_rows, 'grp', split_axis=0, concat_axi...  7.51 us
    dynamic_update_slice x4, local copies, waits for them, and re-layouts, fetched_terms(): weight_table = lax.map(table_one, (code_rows, weight))  7.34 us
    all_to_all x1, blocking collectives, shards(): lax.all_to_all(found_codes, 'grp', split_axis=0, concat_axis=0, tiled=True)  6.5 us
  transfers between devices with their start and end apart: 5, of which 5 were waited for; matrix products, arithmetic and copies ran while one was open for 6% of the time, Pallas kernels for 0%

commit v1 on v0

--- a/solution.py
+++ b/solution.py
@@ -85,12 +85,20 @@
     found_rows = documents[doc_index].reshape(groups, owners, capacity, D)
     found_codes = doc_codes[doc_index].astype(jnp.float32).reshape(groups, owners, capacity, M)
     fetched, fetched_codes = (
-        lax.all_to_all(
-            lax.all_to_all(found_rows, "grp", split_axis=0, concat_axis=0, tiled=True),
-            "dev",
-            split_axis=1,
-            concat_axis=1,
-            tiled=True,
+        jnp.concatenate(
+            lax.all_to_all(
+                jnp.stack(
+                    jnp.split(
+                        lax.all_to_all(found_rows, "grp", split_axis=0, concat_axis=0, tiled=True),
+                        lax.axis_size("dev"),
+                        axis=1,
+                    )
+                ),
+                "dev",
+                0,
+                0,
+            ),
+            axis=1,
         ),
         lax.all_to_all(
             lax.all_to_all(found_codes, "grp", split_axis=0, concat_axis=0, tiled=True),

time: 181 us -> 190 us (1.050)
  local copies, waits for them, and re-layouts: 19.3 us -> 28.1 us
    unnamed x9 -> x24, local copies, waits for them, and re-layouts: 0.35 us -> 9.42 us
where the time goes in v1:
time: 190 us; the launch traced here: 189 us
  waiting for transfers between devices  85.9 us (45%)
  local copies, waits for them, and re-layouts  28.1 us (15%)
  blocking collectives  26.5 us (14%)
  between operations  14.3 us (8%)
  matrix products  11.8 us (6%)
  other arithmetic  11.6 us (6%)
  starting transfers between devices  10.6 us (6%)
    reduce_scatter x1, waiting for transfers between devices, shards(): lax.psum_scatter(local_gradient, 'dev', scatter_dimension=0, tiled=True)  55.9 us
    all_to_all x1, blocking collectives, shards(): lax.all_to_all(lax.all_to_all(wanted.reshape(groups, owners, capacity), '...  12.2 us
    reduce_scatter x1, waiting for transfers between devices, shards(): lax.psum_scatter(partial_sum, 'grp', scatter_dimension=1, tiled=True)  11.7 us
    unnamed x24, local copies, waits for them, and re-layouts  9.42 us
    dot_general x4, matrix products, table_one(): jnp.einsum('cmk,c->mk', code_onehot(code_one), weight_one, precision=lax....  8.72 us
    all_to_all x1, blocking collectives, shards(): lax.all_to_all(wanted.reshape(groups, owners, capacity), 'grp', split_axi...  7.82 us
    all_to_all x1, waiting for transfers between devices, shards(): lax.all_to_all(jnp.stack(jnp.split(lax.all_to_all(found_rows, 'grp', spli...  7.51 us
    dynamic_update_slice x4, local copies, waits for them, and re-layouts, fetched_terms(): weight_table = lax.map(table_one, (code_rows, weight))  7.34 us
  transfers between devices with their start and end apart: 5, of which 5 were waited for; matrix products, arithmetic and copies ran while one was open for 6% of the time, Pallas kernels for 0%

profile of v1, /device:TPU:0, one launch (start us, length us, event | category | flops | bytes accessed | tf_op | source)
XLA Modules:
  0.0 189.0 jit_solution(4928389325548906509)
XLA Ops:
  9.8 1.0 scatter_custom_fusion
  11.0 7.8 %all_to_all.30 = s32[2,16,4]{1,2,0:T(4,128)S(1)} all-to-all(s32[2,16,4]{1,2,0:T(4,128)S(1)} %copy.106), channel_id=1, replica_groups=mesh['grp'=2,'dev'=16] {'grp'}, dimensions={0} | all-to-all | bytes 1024 | tf_op jit(solution)/shard_map/all_to_all | solution.py:76
  18.9 12.2 %all_to_all.31 = s32[2,16,4]{2,0,1:T(2,128)S(1)} all-to-all(s32[2,16,4]{2,0,1:T(2,128)S(1)} %copy.107), channel_id=1, replica_groups=mesh['grp'=2,'dev'=16] {'dev'}, dimensions={1} | all-to-all | bytes 1024 | tf_op jit(solution)/shard_map/all_to_all | solution.py:75
  31.2 1.5 gather_fusion
  32.7 6.5 %all_to_all.32 = f32[2,16,4,128]{3,2,1,0:T(4,128)S(1)} all-to-all(f32[2,16,4,128]{3,2,1,0:T(4,128)S(1)} %bitcast.161), channel_id=1, replica_groups=mesh['grp'=2,'dev'=16] {'grp'}, dimensions={0} | all-to-all | bytes 131072 | tf_op jit(solution)/shard_map/all_to_all | solution.py:104
  39.8 3.5 %all-to-all-start.3 = ((f32[2,16,4,128]{3,2,0,1:T(4,128)}), f32[2,16,4,128]{3,2,0,1:T(4,128)S(1)}, u32[]{:S(2)}, u32[]{:S(2)}) async-start(f32[2,16,4,128]{3,2,0,1:T(4,128)} %copy.109), calls=%async_computation.3 | async-start | bytes 131072 | tf_op jit(solution)/shard_map/all_to_all | solution.py:103
  44.7 1.0 reshape.118
  45.7 4.5 %all-to-all-done.3 = f32[2,16,4,128]{3,2,0,1:T(4,128)S(1)} async-done(((f32[2,16,4,128]{3,2,0,1:T(4,128)}), f32[2,16,4,128]{3,2,0,1:T(4,128)S(1)}, u32[]{:S(2)}, u32[]{:S(2)}) %all-to-all-start.3) | async-done | bytes 65568 | tf_op jit(solution)/shard_map/all_to_all | solution.py:103
  50.2 3.5 %all-to-all-start.4 = ((f32[2,16,4,1024]{3,2,1,0:T(4,128)}), f32[2,16,4,1024]{3,2,1,0:T(4,128)S(1)}, u32[]{:S(2)}, u32[]{:S(2)}) async-start(f32[2,16,4,1024]{3,2,1,0:T(4,128)} %reshape.118), calls=%async_computation.4 | async-start | bytes 1048576 | tf_op jit(solution)/shard_map/all_to_all | solution.py:92
  53.7 1.1 convolution_bitcast_fusion.1
  55.5 6.1 %all-to-all-done.4 = f32[2,16,4,1024]{3,2,1,0:T(4,128)S(1)} async-done(((f32[2,16,4,1024]{3,2,1,0:T(4,128)}), f32[2,16,4,1024]{3,2,1,0:T(4,128)S(1)}, u32[]{:S(2)}, u32[]{:S(2)}) %all-to-all-start.4) | async-done | bytes 524320 | tf_op jit(solution)/shard_map/all_to_all | solution.py:92
  71.3 3.6 %all-to-all-start.5 = ((f32[16,2,1,4,1024]{4,3,1,2,0:T(4,128)}), f32[16,2,1,4,1024]{4,3,1,2,0:T(4,128)S(1)}, u32[]{:S(2)}, u32[]{:S(2)}) async-start(f32[16,2,1,4,1024]{4,3,1,2,0:T(4,128)} %fusion.8), calls=%async_computation.5 | async-start | bytes 1048576 | tf_op jit(solution)/shard_map/all_to_all | solution.py:89
  75.0 6.7 %while.20 = (s32[]{:T(128)}, f32[4,32]{1,0:T(4,128)S(1)}, s32[4,32,128]{2,1,0:T(8,128)S(1)}, f32[4,128,256]{2,0,1:T(4,128)S(1)}, s32[]{:T(128)}, /*index=5*/s32[]{:T(128)}) while((s32[]{:T(128)}, f32[4,32]{1,0:T(4,128)S(1)}, s32[4,32,128]{2,1,0:T(8,128)S(1)}, f32[4,128,256]{2,0,1:T(4,128)S(1)}, s32[]{:T(128)}, /*index=5*/s32[]{:T(128)}) %tuple.53), condition=%wide.region_3.4_spmd, body=%wide.region_2.3_spmd.sunk | while | flops 3145698 | bytes 704977 | solution.py:51
  75.1 1.5 select_reduce_fusion.2
  76.8 1.5 select_reduce_fusion.2
  78.5 1.5 select_reduce_fusion.2
  80.2 1.5 select_reduce_fusion.2
  81.8 7.5 %all-to-all-done.5 = f32[16,2,1,4,1024]{4,3,1,2,0:T(4,128)S(1)} async-done(((f32[16,2,1,4,1024]{4,3,1,2,0:T(4,128)}), f32[16,2,1,4,1024]{4,3,1,2,0:T(4,128)S(1)}, u32[]{:S(2)}, u32[]{:S(2)}) %all-to-all-start.5) | async-done | bytes 524320 | tf_op jit(solution)/shard_map/all_to_all | solution.py:89
  92.0 19.7 %while.21 = (s32[]{:T(128)}, f32[4,128,256]{2,0,1:T(4,128)S(1)}, s32[4,32,128]{2,1,0:T(8,128)S(1)}, f32[4,32]{1,0:T(4,128)S(1)}, s32[]{:T(128)}, /*index=5*/s32[]{:T(128)}) while((s32[]{:T(128)}, f32[4,128,256]{2,0,1:T(4,128)S(1)}, s32[4,32,128]{2,1,0:T(8,128)S(1)}, f32[4,32]{1,0:T(4,128)S(1)}, s32[]{:T(128)}, /*index=5*/s32[]{:T(128)}) %tuple.55), condition=%wide.region_9.10_spmd, body=%wide.region_8.9_spmd.sunk | while | flops 13631490 | bytes 2540113 | solution.py:60
  92.9 2.2 %fusion.37 = f32[1,128,256]{2,0,1:T(1,128)S(1)} fusion(pred[32,128,256]{2,1,0:T(32,128)(4,1)S(1)} %iota_compare_fusion.4, f32[4,32]{1,0:T(4,128)S(1)} %get-tuple-element.172, s32[]{:T(128)} %get-tuple-element.163), kind=kOutput, calls=%fused_computation.6.clone.1 | convolution fusion | flops 12582912 | bytes 1180164 | tf_op jit(solution)/shard_map/while/body/eval_jaxpr/cmk,c->mk/dot_general | solution.py:56
  95.1 1.8 dynamic_update_slice.11
  97.8 2.2 %fusion.37 = f32[1,128,256]{2,0,1:T(1,128)S(1)} fusion(pred[32,128,256]{2,1,0:T(32,128)(4,1)S(1)} %iota_compare_fusion.4, f32[4,32]{1,0:T(4,128)S(1)} %get-tuple-element.172, s32[]{:T(128)} %get-tuple-element.163), kind=kOutput, calls=%fused_computation.6.clone.1 | convolution fusion | flops 12582912 | bytes 1180164 | tf_op jit(solution)/shard_map/while/body/eval_jaxpr/cmk,c->mk/dot_general | solution.py:56
  100.0 1.8 dynamic_update_slice.11
  102.8 2.2 %fusion.37 = f32[1,128,256]{2,0,1:T(1,128)S(1)} fusion(pred[32,128,256]{2,1,0:T(32,128)(4,1)S(1)} %iota_compare_fusion.4, f32[4,32]{1,0:T(4,128)S(1)} %get-tuple-element.172, s32[]{:T(128)} %get-tuple-element.163), kind=kOutput, calls=%fused_computation.6.clone.1 | convolution fusion | flops 12582912 | bytes 1180164 | tf_op jit(solution)/shard_map/while/body/eval_jaxpr/cmk,c->mk/dot_general | solution.py:56
  104.9 1.8 dynamic_update_slice.11
  106.8 0.9 iota_compare_fusion.4
  107.7 2.2 %fusion.37 = f32[1,128,256]{2,0,1:T(1,128)S(1)} fusion(pred[32,128,256]{2,1,0:T(32,128)(4,1)S(1)} %iota_compare_fusion.4, f32[4,32]{1,0:T(4,128)S(1)} %get-tuple-element.172, s32[]{:T(128)} %get-tuple-element.163), kind=kOutput, calls=%fused_computation.6.clone.1 | convolution fusion | flops 12582912 | bytes 1180164 | tf_op jit(solution)/shard_map/while/body/eval_jaxpr/cmk,c->mk/dot_general | solution.py:56
  109.9 1.8 dynamic_update_slice.11
  111.7 1.4 convolution_bitcast_fusion
  113.1 1.3 copy.132
  114.5 55.9 %reduce-scatter.3.cloned.1.call-done = f32[16,1024]{1,0:T(8,128)} async-done(((f32[256,1024]{1,0:T(8,128)}), f32[16,1024]{1,0:T(8,128)}) %reduce-scatter.3.cloned.1.call-update) | async-done | bytes 65552 | tf_op jit(solution)/shard_map/reduce_scatter | solution.py:116
  170.5 11.7 %reduce-scatter.5.cloned.1.call-done = f32[16,512]{1,0:T(8,128)} async-done(((f32[16,1024]{1,0:T(8,128)}), f32[16,512]{1,0:T(8,128)}) %reduce-scatter.5.cloned.1.call-update) | async-done | bytes 32784 | tf_op jit(solution)/shard_map/reduce_scatter | solution.py:117
  (85 shorter events, 21.4 us)
Async XLA Ops:
  7.2 36.7 %copy-start = (f32[128,1024]{1,0:T(8,128)S(1)}, f32[128,1024]{1,0:T(8,128)}, u32[]{:S(2)}) copy-start(f32[128,1024]{1,0:T(8,128)} %param.12) | copy-start | bytes 1572868
  7.2 36.2 %copy-start.3 = (f32[4,1024]{1,0:T(4,128)S(1)}, f32[4,1024]{1,0:T(4,128)}, u32[]{:S(2)}) copy-start(f32[4,1024]{1,0:T(4,128)} %param.11) | copy-start | bytes 49156
  7.2 36.4 %copy-start.1 = (f32[256,1024]{1,0:T(8,128)S(1)}, f32[256,1024]{1,0:T(8,128)}, u32[]{:S(2)}) copy-start(f32[256,1024]{1,0:T(8,128)} %param.14) | copy-start | bytes 3145732
  39.8 10.4 %all-to-all-start.3 = ((f32[2,16,4,128]{3,2,0,1:T(4,128)}), f32[2,16,4,128]{3,2,0,1:T(4,128)S(1)}, u32[]{:S(2)}, u32[]{:S(2)}) async-start(f32[2,16,4,128]{3,2,0,1:T(4,128)} %copy.109), calls=%async_computation.3 | async-start | bytes 131072 | tf_op jit(solution)/shard_map/all_to_all | solution.py:103
  50.2 11.5 %all-to-all-start.4 = ((f32[2,16,4,1024]{3,2,1,0:T(4,128)}), f32[2,16,4,1024]{3,2,1,0:T(4,128)S(1)}, u32[]{:S(2)}, u32[]{:S(2)}) async-start(f32[2,16,4,1024]{3,2,1,0:T(4,128)} %reshape.118), calls=%async_computation.4 | async-start | bytes 1048576 | tf_op jit(solution)/shard_map/all_to_all | solution.py:92
  71.3 18.0 %all-to-all-start.5 = ((f32[16,2,1,4,1024]{4,3,1,2,0:T(4,128)}), f32[16,2,1,4,1024]{4,3,1,2,0:T(4,128)S(1)}, u32[]{:S(2)}, u32[]{:S(2)}) async-start(f32[16,2,1,4,1024]{4,3,1,2,0:T(4,128)} %fusion.8), calls=%async_computation.5 | async-start | bytes 1048576 | tf_op jit(solution)/shard_map/all_to_all | solution.py:89
  74.9 95.5 %reduce-scatter.3.cloned.1.call-start = ((), (), s32[]{:S(2)}) async-start(), calls=%async_computation.8 | async-start | bytes 1114112 | tf_op jit(solution)/shard_map/reduce_scatter | solution.py:116
  89.6 2.5 %copy-start.2 = (f32[4,128,256]{2,0,1:T(4,128)S(1)}, f32[4,128,256]{2,0,1:T(4,128)}, u32[]{:S(2)}) copy-start(f32[4,128,256]{2,0,1:T(4,128)} %custom-call.10) | copy-start | bytes 1572868
  114.4 67.8 %reduce-scatter.5.cloned.1.call-start = ((), (), s32[]{:S(2)}) async-start(), calls=%async_computation.9 | async-start | bytes 98304 | tf_op jit(solution)/shard_map/reduce_scatter | solution.py:117
Sparse Core Ops, SparseCore 0:
  114.6 55.8 reduce-scatter.2
  173.3 8.8 reduce-scatter.4
